TPU v7x, 32 devices: a whole 2x2x4 slice. The times are simulated.
32 devices in a mesh: dp: 8 (over z, core), tensor: 4 (over y, x).
Axes of the slice: x: 2, y: 2, z: 4, core: 2. Of those that a mesh axis runs over, the one named last changes fastest.
Arguments:
- inputs: bfloat16 [8192, 2048], P(('dp', 'tensor')), may hold values from -6 to 6
- teacher: bfloat16 [8192, 2048], P(('dp', 'tensor')), may hold values from -6 to 6
- segment: int32 [8192], P('dp'), may hold values from 0 to 13, as said below
- position: int32 [8192], P('dp'), may hold values from 0 to 1023, as said below
- wq: bfloat16 [2048, 2048], P('dp', 'tensor'), may hold values from -0.125 to 0.125
- wk: bfloat16 [2048, 2048], P('dp', 'tensor'), may hold values from -0.125 to 0.125
- wv: bfloat16 [2048, 2048], P('dp', 'tensor'), may hold values from -0.125 to 0.125
- wo: bfloat16 [2048, 2048], P('tensor', 'dp'), may hold values from -0.125 to 0.125
- wg: bfloat16 [2048, 8192], P('dp', 'tensor'), may hold values from -0.125 to 0.125
- wu: bfloat16 [2048, 8192], P('dp', 'tensor'), may hold values from -0.125 to 0.125
- wd: bfloat16 [8192, 2048], P('tensor', 'dp'), may hold values from -0.0625 to 0.0625
- q_gain: bfloat16 [2048], P('dp'), may hold values from 0.099609375 to 1.8984375
- k_gain: bfloat16 [2048], P('dp'), may hold values from 0.099609375 to 1.8984375
- attn_gain: bfloat16 [2048], P('dp'), may hold values from 0.099609375 to 1.8984375
- ffn_gain: bfloat16 [2048], P('dp'), may hold values from 0.099609375 to 1.8984375
Outputs:
- output: bfloat16 [8192, 2048], P(('dp', 'tensor'))
- loss: float32 [], replicated
- grad_x: float32 [8192, 2048], P(('dp', 'tensor'))
- grad_wq: float32 [2048, 2048], P('dp', 'tensor')
- grad_wk: float32 [2048, 2048], P('dp', 'tensor')
- grad_wv: float32 [2048, 2048], P('dp', 'tensor')
- grad_wo: float32 [2048, 2048], P('tensor', 'dp')
- grad_wg: float32 [2048, 8192], P('dp', 'tensor')
- grad_wu: float32 [2048, 8192], P('dp', 'tensor')
- grad_wd: float32 [8192, 2048], P('tensor', 'dp')
- grad_q_gain: float32 [2048], P('dp')
- grad_k_gain: float32 [2048], P('dp')
- grad_attn_gain: float32 [2048], P('dp')
- grad_ffn_gain: float32 [2048], P('dp')
Inputs may be any that keep to these rules, and one draw needn't show every extreme that they name: `segment`: each sequence is 1024 consecutive tokens; in it, documents are runs of one nonzero number that never falls, followed at the sequence's end by a run of zeros (padding), which may be empty. Numbers repeat in other sequences. Sequence 0 is one whole document; sequence 1 holds thirteen. `position`: each token's index within its document; padding tokens count from the start of their padding run.
All inputs are finite; a program needn't handle non-finite values.
Results may differ from a plain program's by a relative error of at most 0.025.
Values may be sent and summed in bfloat16 or wider, within the bound.
No kernel may reach another device: no remote copies, remote signals or barrier semaphores. Data moves between devices by JAX's collectives and lax.ppermute only.
A program may use at most 192 MiB of HBM per device.

v0:
```python
import jax
import jax.numpy as jnp
from jax import lax
from jax.sharding import PartitionSpec as P

HD = 128
LEN = 1024
EPS = 1e-06
THETA = 500000.0
NEGATIVE = -1e30


def tables(position):
    freq = 1.0 / THETA ** (jnp.arange(0, HD, 2).astype(jnp.float32) / HD)
    angle = position.astype(jnp.float32)[:, None] * freq[None, :]
    angle = jnp.concatenate([angle, angle], axis=1)[:, None, :]
    return (jnp.cos(angle), jnp.sin(angle))


def rotate(values, cosines, sines):
    half = values.shape[-1] // 2
    turned = jnp.concatenate([-values[..., half:], values[..., :half]], axis=-1)
    return values * cosines + turned * sines


def unrotate(grad, cosines, sines):
    half = grad.shape[-1] // 2
    turned = grad * sines
    return grad * cosines + jnp.concatenate([turned[..., half:], -turned[..., :half]], axis=-1)


def inner_rows(left, right):
    return lax.dot_general(
        left, right, (((0,), (0,)), ((), ())), preferred_element_type=jnp.float32
    )


def times_transposed(left, right):
    return lax.dot_general(
        left, right, (((1,), (1,)), ((), ())), preferred_element_type=jnp.float32
    )


def allowed_keys(segment):
    length = segment.shape[0]
    place = lax.broadcasted_iota(jnp.int32, (length, length), 0)
    other = lax.broadcasted_iota(jnp.int32, (length, length), 1)
    return (segment[:, None] == segment[None, :]) & (place >= other)


def masked_scores(query, key, segment):
    scores = jnp.einsum(
        "qhd,khd->hqk", query, key, preferred_element_type=jnp.float32
    ) * query.shape[-1] ** (-0.5)
    return jnp.where(allowed_keys(segment)[None], scores, NEGATIVE)


def attend_forward(pack):
    query, key, value, segment = pack
    scores = masked_scores(query, key, segment)
    highest = jnp.max(scores, axis=-1, keepdims=True)
    raised = jnp.exp(scores - highest)
    total = jnp.sum(raised, axis=-1, keepdims=True)
    prob = (raised / total).astype(jnp.bfloat16)
    mixed = jnp.einsum("hqk,khd->qhd", prob, value, preferred_element_type=jnp.float32)
    return (mixed.astype(jnp.bfloat16), (highest + jnp.log(total))[..., 0])


def attend_backward(pack):
    query, key, value, segment, logsum, grad_mixed = pack
    scores = masked_scores(query, key, segment)
    prob = jnp.exp(scores - logsum[..., None])
    grad_prob = jnp.einsum("qhd,khd->hqk", grad_mixed, value, preferred_element_type=jnp.float32)
    delta = jnp.sum(grad_prob * prob, axis=-1, keepdims=True)
    grad_scores = (prob * (grad_prob - delta)).astype(jnp.bfloat16)
    factor = query.shape[-1] ** (-0.5)
    grad_value = jnp.einsum(
        "hqk,qhd->khd", prob.astype(jnp.bfloat16), grad_mixed, preferred_element_type=jnp.float32
    )
    grad_query = (
        jnp.einsum("hqk,khd->qhd", grad_scores, key, preferred_element_type=jnp.float32) * factor
    )
    grad_key = (
        jnp.einsum("hqk,qhd->khd", grad_scores, query, preferred_element_type=jnp.float32) * factor
    )
    return (grad_query, grad_key, grad_value.astype(jnp.bfloat16))


def reduce_ffn(weight_gate, weight_up, weight_down):
    return (
        lax.psum_scatter(
            weight_gate.astype(jnp.bfloat16), "dp", scatter_dimension=0, tiled=True
        ).astype(jnp.float32),
        lax.psum_scatter(
            weight_up.astype(jnp.bfloat16), "dp", scatter_dimension=0, tiled=True
        ).astype(jnp.float32),
        lax.psum_scatter(
            weight_down.astype(jnp.bfloat16), "dp", scatter_dimension=1, tiled=True
        ).astype(jnp.float32),
    )


def on_device(
    inputs,
    teacher,
    segment,
    position,
    wq,
    wk,
    wv,
    wo,
    wg,
    wu,
    wd,
    q_gain,
    k_gain,
    attn_gain,
    ffn_gain,
):
    gathered = (
        lax.all_gather(wq, "dp", axis=0, tiled=True),
        lax.all_gather(wk, "dp", axis=0, tiled=True),
        lax.all_gather(wv, "dp", axis=0, tiled=True),
        lax.all_gather(wo, "dp", axis=1, tiled=True),
        lax.all_gather(wg, "dp", axis=0, tiled=True),
        lax.all_gather(wu, "dp", axis=0, tiled=True),
        lax.all_gather(wd, "dp", axis=1, tiled=True),
        lax.all_gather(q_gain, "dp", axis=0, tiled=True),
        lax.all_gather(k_gain, "dp", axis=0, tiled=True),
        lax.all_gather(attn_gain, "dp", axis=0, tiled=True),
        lax.all_gather(ffn_gain, "dp", axis=0, tiled=True),
    )
    (
        full_q,
        full_k,
        full_v,
        full_out,
        full_gate,
        full_up,
        full_down,
        gain_q,
        gain_k,
        gain_attn,
        gain_ffn,
    ) = gathered
    rows, width = inputs.shape
    local_width = full_q.shape[1]
    heads_here = local_width // HD
    offset = lax.axis_index("tensor") * local_width
    local_gain_q = lax.dynamic_slice_in_dim(gain_q, offset, local_width).astype(jnp.float32)
    local_gain_k = lax.dynamic_slice_in_dim(gain_k, offset, local_width).astype(jnp.float32)
    norm_gain_attn = gain_attn.astype(jnp.float32)
    norm_gain_ffn = gain_ffn.astype(jnp.float32)
    cosines, sines = tables(position)
    group = segment.shape[0]
    sequences = group // LEN
    blocks = (sequences, LEN, heads_here, HD)
    segments = segment.reshape(sequences, LEN)
    whole_inputs = lax.all_gather(inputs, "tensor", axis=0, tiled=True)
    raw_q = jnp.dot(whole_inputs, full_q, preferred_element_type=jnp.float32)
    raw_k = jnp.dot(whole_inputs, full_k, preferred_element_type=jnp.float32)
    value = (
        jnp.dot(whole_inputs, full_v, preferred_element_type=jnp.float32)
        .astype(jnp.bfloat16)
        .reshape(blocks)
    )
    square_q, square_k = lax.psum(
        (jnp.sum(raw_q * raw_q, axis=1), jnp.sum(raw_k * raw_k, axis=1)), "tensor"
    )
    scale_q = lax.rsqrt(square_q / width + EPS)[:, None]
    scale_k = lax.rsqrt(square_k / width + EPS)[:, None]
    normed_q = raw_q * scale_q
    normed_k = raw_k * scale_k
    query = (
        rotate((normed_q * local_gain_q).reshape(group, heads_here, HD), cosines, sines)
        .astype(jnp.bfloat16)
        .reshape(blocks)
    )
    key = (
        rotate((normed_k * local_gain_k).reshape(group, heads_here, HD), cosines, sines)
        .astype(jnp.bfloat16)
        .reshape(blocks)
    )
    mixed, logsum = lax.map(attend_forward, (query, key, value, segments))
    attn_rows = mixed.reshape(group, local_width)
    branch_attn = lax.psum_scatter(
        jnp.dot(attn_rows, full_out, preferred_element_type=jnp.float32).astype(jnp.bfloat16),
        "tensor",
        scatter_dimension=0,
        tiled=True,
    ).astype(jnp.float32)
    scale_attn = lax.rsqrt(jnp.mean(branch_attn * branch_attn, axis=1, keepdims=True) + EPS)
    normed_attn = branch_attn * scale_attn
    resid = inputs.astype(jnp.float32) + normed_attn * norm_gain_attn
    whole_h = lax.all_gather(resid.astype(jnp.bfloat16), "tensor", axis=0, tiled=True)
    gate = jnp.dot(whole_h, full_gate, preferred_element_type=jnp.float32)
    up = jnp.dot(whole_h, full_up, preferred_element_type=jnp.float32)
    sigma = jax.nn.sigmoid(gate)
    activated = gate * sigma
    hidden = (activated * up).astype(jnp.bfloat16)
    branch_ffn = lax.psum_scatter(
        jnp.dot(hidden, full_down, preferred_element_type=jnp.float32).astype(jnp.bfloat16),
        "tensor",
        scatter_dimension=0,
        tiled=True,
    ).astype(jnp.float32)
    scale_ffn = lax.rsqrt(jnp.mean(branch_ffn * branch_ffn, axis=1, keepdims=True) + EPS)
    normed_ffn = branch_ffn * scale_ffn
    output = resid + normed_ffn * norm_gain_ffn
    my_segment = lax.dynamic_slice_in_dim(segment, lax.axis_index("tensor") * rows, rows)
    valid = (my_segment != 0).astype(jnp.float32)[:, None]
    error = output - teacher.astype(jnp.float32)
    loss_total, valid_total = lax.psum(
        (jnp.sum(valid * error * error), jnp.sum(valid)), ("dp", "tensor")
    )
    loss = loss_total / (valid_total * width)
    tokens_all = rows * lax.axis_size("dp") * lax.axis_size("tensor")
    grad_output = 2.0 * tokens_all * valid * error / valid_total
    grad_gain_ffn = jnp.sum(grad_output * normed_ffn, axis=0)
    grad_normed = grad_output * norm_gain_ffn
    grad_branch_ffn = (
        scale_ffn
        * (grad_normed - normed_ffn * jnp.mean(grad_normed * normed_ffn, axis=1, keepdims=True))
    ).astype(jnp.bfloat16)
    piece = lax.all_gather(grad_branch_ffn, "tensor", axis=0, tiled=True)
    grad_down = inner_rows(hidden, piece)
    grad_hidden = times_transposed(piece, full_down)
    grad_down, grad_hidden = (grad_down, grad_hidden)
    grad_gate = (grad_hidden * up * sigma * (1.0 + gate * (1.0 - sigma))).astype(jnp.bfloat16)
    grad_up = (grad_hidden * activated).astype(jnp.bfloat16)
    weight_gate = inner_rows(whole_h, grad_gate)
    weight_up = inner_rows(whole_h, grad_up)
    grad_resid = grad_output + lax.psum_scatter(
        (times_transposed(grad_gate, full_gate) + times_transposed(grad_up, full_up)).astype(
            jnp.bfloat16
        ),
        "tensor",
        scatter_dimension=0,
        tiled=True,
    ).astype(jnp.float32)
    ffn_sums = None
    grad_gain_attn = jnp.sum(grad_resid * normed_attn, axis=0)
    grad_normed = grad_resid * norm_gain_attn
    grad_branch_attn = (
        scale_attn
        * (grad_normed - normed_attn * jnp.mean(grad_normed * normed_attn, axis=1, keepdims=True))
    ).astype(jnp.bfloat16)
    piece = lax.all_gather(grad_branch_attn, "tensor", axis=0, tiled=True)
    grad_out_weight = inner_rows(attn_rows, piece)
    grad_mixed = times_transposed(piece, full_out)
    grad_out_weight, grad_mixed = (grad_out_weight, grad_mixed)
    grad_mixed = grad_mixed.astype(jnp.bfloat16).reshape(blocks)
    grad_query, grad_key, grad_value = lax.map(
        attend_backward, (query, key, value, segments, logsum, grad_mixed)
    )
    grad_normed_q = unrotate(grad_query.reshape(group, heads_here, HD), cosines, sines).reshape(
        group, local_width
    )
    grad_normed_k = unrotate(grad_key.reshape(group, heads_here, HD), cosines, sines).reshape(
        group, local_width
    )
    grad_value = grad_value.reshape(group, local_width)
    grad_hat_q = grad_normed_q * local_gain_q
    grad_hat_k = grad_normed_k * local_gain_k
    placed_q = lax.dynamic_update_slice_in_dim(
        jnp.zeros((width,), jnp.float32), jnp.sum(grad_normed_q * normed_q, axis=0), offset, 0
    )
    placed_k = lax.dynamic_update_slice_in_dim(
        jnp.zeros((width,), jnp.float32), jnp.sum(grad_normed_k * normed_k, axis=0), offset, 0
    )
    gain_rows = jnp.stack([placed_q, placed_k, grad_gain_attn, grad_gain_ffn])
    inner_q, inner_k, gain_rows = (
        lax.psum(jnp.sum(grad_hat_q * normed_q, axis=1).astype(jnp.bfloat16), "tensor").astype(
            jnp.float32
        ),
        lax.psum(jnp.sum(grad_hat_k * normed_k, axis=1).astype(jnp.bfloat16), "tensor").astype(
            jnp.float32
        ),
        lax.psum(gain_rows.astype(jnp.bfloat16), "tensor").astype(jnp.float32),
    )
    grad_raw_q = (scale_q * (grad_hat_q - normed_q * (inner_q / width)[:, None])).astype(
        jnp.bfloat16
    )
    grad_raw_k = (scale_k * (grad_hat_k - normed_k * (inner_k / width)[:, None])).astype(
        jnp.bfloat16
    )
    weight_q = inner_rows(whole_inputs, grad_raw_q)
    weight_k = inner_rows(whole_inputs, grad_raw_k)
    weight_v = inner_rows(whole_inputs, grad_value)
    grad_input = grad_resid + lax.psum_scatter(
        (
            times_transposed(grad_raw_q, full_q)
            + times_transposed(grad_raw_k, full_k)
            + times_transposed(grad_value, full_v)
        ).astype(jnp.bfloat16),
        "tensor",
        scatter_dimension=0,
        tiled=True,
    ).astype(jnp.float32)
    ffn_sums = reduce_ffn(weight_gate, weight_up, grad_down)
    attn_sums = (
        lax.psum_scatter(
            weight_q.astype(jnp.bfloat16), "dp", scatter_dimension=0, tiled=True
        ).astype(jnp.float32),
        lax.psum_scatter(
            weight_k.astype(jnp.bfloat16), "dp", scatter_dimension=0, tiled=True
        ).astype(jnp.float32),
        lax.psum_scatter(
            weight_v.astype(jnp.bfloat16), "dp", scatter_dimension=0, tiled=True
        ).astype(jnp.float32),
        lax.psum_scatter(
            grad_out_weight.astype(jnp.bfloat16), "dp", scatter_dimension=1, tiled=True
        ).astype(jnp.float32),
        lax.psum_scatter(
            gain_rows.astype(jnp.bfloat16), "dp", scatter_dimension=1, tiled=True
        ).astype(jnp.float32),
    )
    gains_done = attn_sums[4]
    return (
        output.astype(jnp.bfloat16),
        loss,
        grad_input,
        attn_sums[0],
        attn_sums[1],
        attn_sums[2],
        attn_sums[3],
        ffn_sums[0],
        ffn_sums[1],
        ffn_sums[2],
        gains_done[0],
        gains_done[1],
        gains_done[2],
        gains_done[3],
    )


def solution(mesh):
    placed = (
        P(("dp", "tensor"), None),
        P(("dp", "tensor"), None),
        P("dp"),
        P("dp"),
        P("dp", "tensor"),
        P("dp", "tensor"),
        P("dp", "tensor"),
        P("tensor", "dp"),
        P("dp", "tensor"),
        P("dp", "tensor"),
        P("tensor", "dp"),
        P("dp"),
        P("dp"),
        P("dp"),
        P("dp"),
    )
    return jax.shard_map(
        on_device,
        mesh=mesh,
        in_specs=placed,
        out_specs=(
            P(("dp", "tensor"), None),
            P(),
            P(("dp", "tensor"), None),
            P("dp", "tensor"),
            P("dp", "tensor"),
            P("dp", "tensor"),
            P("tensor", "dp"),
            P("dp", "tensor"),
            P("dp", "tensor"),
            P("tensor", "dp"),
            P("dp"),
            P("dp"),
            P("dp"),
            P("dp"),
        ),
        check_vma=False,
    )
```

profile of v0, /device:TPU:0, one launch (start us, length us, event | category | flops | bytes accessed | tf_op | source)
XLA Modules:
  0.0 1392.0 jit_solution(2718220709139810881)
XLA Ops:
  10.7 13.5 all-gather.1
  27.2 9.1 all-gather
  41.6 53.8 %all-gather.16.cloned.1.call-done = bf16[1024,2048]{1,0:T(8,128)(2,1)} async-done(((bf16[256,2048]{1,0:T(8,128)(2,1)}), bf16[1024,2048]{1,0:T(8,128)(2,1)}) %all-gather.16.cloned.1.call-update) | async-done | bytes 4194320 | tf_op jit(solution)/shard_map/all_gather | solution.py:159
  95.4 5.3 multiply_reduce_fusion.3
  100.7 25.5 %all-gather.20.cloned.1.call-done = bf16[2048,512]{1,0:T(8,128)(2,1)} async-done(((bf16[256,512]{1,0:T(8,128)(2,1)}), bf16[2048,512]{1,0:T(8,128)(2,1)}) %all-gather.20.cloned.1.call-update) | async-done | bytes 2097168 | tf_op jit(solution)/shard_map/all_gather | solution.py:121
  126.2 6.6 multiply_reduce_fusion.4
  132.8 10.0 all-reduce
  149.0 7.8 fusion.52
  162.0 8.7 fusion
  171.3 7.7 fusion.41
  179.1 8.6 all-gather.24.cloned.1.call-done
  187.7 6.0 convolution_convert_fusion.4
  194.6 11.7 all-gather.2
  206.3 39.3 %reduce-scatter.15.cloned.1.call-done = bf16[256,2048]{1,0:T(8,128)(2,1)} async-done(((bf16[1024,2048]{1,0:T(8,128)(2,1)}), bf16[256,2048]{1,0:T(8,128)(2,1)}) %reduce-scatter.15.cloned.1.call-update) | async-done | bytes 1048592 | tf_op jit(solution)/shard_map/reduce_scatter | solution.py:186
  251.1 78.1 %all-gather.28.cloned.1.call-done = bf16[2048,2048]{1,0:T(8,128)(2,1)} async-done(((bf16[256,2048]{1,0:T(8,128)(2,1)}), bf16[2048,2048]{1,0:T(8,128)(2,1)}) %all-gather.28.cloned.1.call-update) | async-done | bytes 8388624 | tf_op jit(solution)/shard_map/all_gather | solution.py:125
  329.2 53.5 %all-gather.26.cloned.1.call-done = bf16[1024,2048]{1,0:T(8,128)(2,1)} async-done(((bf16[256,2048]{1,0:T(8,128)(2,1)}), bf16[1024,2048]{1,0:T(8,128)(2,1)}) %all-gather.26.cloned.1.call-update) | async-done | bytes 4194320 | tf_op jit(solution)/shard_map/all_gather | solution.py:195
  382.7 14.8 %fusion.53 = f32[1024,2048]{1,0:T(8,128)} fusion(bf16[1024,2048]{1,0:T(8,128)(2,1)} %all-gather.26.cloned.1.call-done, bf16[2048,2048]{1,0:T(8,128)(2,1)} %all-gather.28.cloned.1.call-done), kind=kOutput, calls=%fused_computation.129 | convolution fusion | flops 8589934592 | bytes 20971520 | tf_op jit(solution)/shard_map/dot_general | solution.py:196
  397.5 68.9 %all-gather.30.cloned.1.call-done = bf16[2048,2048]{1,0:T(8,128)(2,1)} async-done(((bf16[256,2048]{1,0:T(8,128)(2,1)}), bf16[2048,2048]{1,0:T(8,128)(2,1)}) %all-gather.30.cloned.1.call-update) | async-done | bytes 8388624 | tf_op jit(solution)/shard_map/all_gather | solution.py:126
  466.4 16.9 %multiply_convert_fusion.3 = (bf16[1024,2048]{1,0:T(8,128)(2,1)}, f32[1024,2048]{1,0:T(8,128)}) fusion(f32[1024,2048]{1,0:T(8,128)} %fusion.53, bf16[1024,2048]{1,0:T(8,128)(2,1)} %all-gather.26.cloned.1.call-done, bf16[2048,2048]{1,0:T(8,128)(2,1)} %all-gather.30.cloned.1.call-done), kind=kOutput, calls=%fused_computation.14 | convolution fusion | flops 8602517504 | bytes 33554432 | tf_op jit(solution)/shard_map/dot_general | solution.py:197
  483.3 65.5 %all-gather.32.cloned.1.call-done = bf16[2048,2048]{1,0:T(8,128)(2,1)} async-done(((bf16[2048,256]{1,0:T(8,128)(2,1)}), bf16[2048,2048]{1,0:T(8,128)(2,1)}) %all-gather.32.cloned.1.call-update) | async-done | bytes 8388624 | tf_op jit(solution)/shard_map/all_gather | solution.py:127
  548.8 13.8 convolution_convert_fusion.3
  563.4 39.7 %psum.52 = f32[]{:T(128)} all-reduce(f32[]{:T(128)} %get-tuple-element.150), channel_id=1, replica_groups=mesh['dp'=8,'tensor'=4] {'dp','tensor'}, use_global_device_ids=true, to_apply=%region_13.14 | all-reduce | flops 1 | bytes 8 | tf_op jit(solution)/shard_map/psum | solution.py:213
  603.1 10.7 all-gather.3
  616.0 5.8 fusion.31
  623.5 52.5 %all-gather.34.cloned.1.call-done = bf16[1024,2048]{1,0:T(8,128)(2,1)} async-done(((bf16[256,2048]{1,0:T(8,128)(2,1)}), bf16[1024,2048]{1,0:T(8,128)(2,1)}) %all-gather.34.cloned.1.call-update) | async-done | bytes 4194320 | tf_op jit(solution)/shard_map/all_gather | solution.py:225
  676.0 20.5 %multiply_convert_fusion.1 = (bf16[1024,2048]{1,0:T(8,128)(2,1)}, bf16[1024,2048]{1,0:T(8,128)(2,1)}) fusion(f32[1024,2048]{1,0:T(8,128)} %fusion.53, f32[1024,2048]{1,0:T(8,128)} %get-tuple-element.158, bf16[1024,2048]{1,0:T(8,128)(2,1)} %all-gather.34.cloned.1.call-done, bf16[2048,2048]{1,0:T(8,128)(2,1)} %all-gather.32.cloned.1.call-done), kind=kOutput, calls=%fused_computation.12 | convolution fusion | flops 8617197568 | bytes 37748736 | tf_op jit(solution)/shard_map/dot_general | solution.py:39
  696.5 12.7 fusion.54
  709.2 13.1 add_convert_fusion.1
  722.3 52.7 %reduce-scatter.19.cloned.1.call-done = bf16[256,2048]{1,0:T(8,128)(2,1)} async-done(((bf16[1024,2048]{1,0:T(8,128)(2,1)}), bf16[256,2048]{1,0:T(8,128)(2,1)}) %reduce-scatter.19.cloned.1.call-update) | async-done | bytes 1048592 | tf_op jit(solution)/shard_map/reduce_scatter | solution.py:233
  780.7 50.8 %all-gather.36.cloned.1.call-done = bf16[1024,2048]{1,0:T(8,128)(2,1)} async-done(((bf16[256,2048]{1,0:T(8,128)(2,1)}), bf16[1024,2048]{1,0:T(8,128)(2,1)}) %all-gather.36.cloned.1.call-update) | async-done | bytes 4194320 | tf_op jit(solution)/shard_map/all_gather | solution.py:248
  836.8 14.5 %multiply_reduce_fusion = (f32[4,1024]{1,0:T(4,128)}, f32[4,1024,1024]{1,2,0:T(8,128)}) fusion(f32[4,1024,1024]{1,2,0:T(8,128)} %get-tuple-element.156, f32[4,1024]{1,0:T(4,128)} %log_add_fusion, bf16[1024,4,128]{0,2,1:T(8,128)(2,1)S(1)} %bitcast.116, bf16[1024,4,128]{0,2,1:T(8,128)(2,1)} %bitcast.121), kind=kOutput, calls=%fused_computation.1 | convolution fusion | flops 1086320640 | bytes 35684352 | tf_op jit(solution)/shard_map/while/body/eval_jaxpr/qhd,khd->hqk/dot_general | solution.py:73
  853.6 8.0 multiply_convert_fusion
  864.9 6.4 bitcast_multiply_fusion.2
  877.8 14.3 %convolution_convert_fusion.2 = bf16[2048,2048]{1,0:T(8,128)(2,1)} fusion(bf16[1024,2048]{1,0:T(8,128)(2,1)} %all-gather.26.cloned.1.call-done, bf16[1024,2048]{1,0:T(8,128)(2,1)} %get-tuple-element.125), kind=kOutput, calls=%fused_computation.20 | convolution fusion | flops 8594128896 | bytes 16777216 | tf_op jit(solution)/shard_map/dot_general | solution.py:33
  892.2 14.0 %convolution_convert_fusion.1 = bf16[2048,2048]{1,0:T(8,128)(2,1)} fusion(bf16[1024,2048]{1,0:T(8,128)(2,1)} %all-gather.26.cloned.1.call-done, bf16[1024,2048]{1,0:T(8,128)(2,1)} %get-tuple-element.124), kind=kOutput, calls=%fused_computation.19 | convolution fusion | flops 8594128896 | bytes 16777216 | tf_op jit(solution)/shard_map/dot_general | solution.py:33
  906.3 14.6 %convolution_convert_fusion = bf16[2048,2048]{1,0:T(8,128)(2,1)} fusion(bf16[1024,2048]{1,0:T(8,128)(2,1)} %get-tuple-element.157, bf16[1024,2048]{1,0:T(8,128)(2,1)} %all-gather.34.cloned.1.call-done), kind=kOutput, calls=%fused_computation.18 | convolution fusion | flops 8594128896 | bytes 16777216 | tf_op jit(solution)/shard_map/dot_general | solution.py:33
  921.6 9.1 fusion.42
  936.7 6.0 convolution_convert_fusion.5
  943.7 9.2 all-reduce.1
  973.9 6.0 add_convert_fusion
  980.6 40.1 %psum.51 = f32[]{:T(128)} all-reduce(f32[]{:T(128)} %get-tuple-element.115), channel_id=1, replica_groups=mesh['dp'=8,'tensor'=4] {'dp','tensor'}, use_global_device_ids=true, to_apply=%region_11.12 | all-reduce | flops 1 | bytes 8 | tf_op jit(solution)/shard_map/psum | solution.py:213
  1024.8 64.7 %reduce-scatter.33.cloned.1.call-done = bf16[256,2048]{1,0:T(8,128)(2,1)} async-done(((bf16[2048,2048]{1,0:T(8,128)(2,1)}), bf16[256,2048]{1,0:T(8,128)(2,1)}) %reduce-scatter.33.cloned.1.call-update) | async-done | bytes 1048592 | tf_op jit(solution)/shard_map/reduce_scatter | solution.py:94
  1092.3 87.1 %reduce-scatter.35.cloned.1.call-done = bf16[2048,256]{1,0:T(8,128)(2,1)} async-done(((bf16[2048,2048]{1,0:T(8,128)(2,1)}), bf16[2048,256]{1,0:T(8,128)(2,1)}) %reduce-scatter.35.cloned.1.call-update) | async-done | bytes 1048592 | tf_op jit(solution)/shard_map/reduce_scatter | solution.py:97
  1182.1 34.0 %reduce-scatter.27.cloned.1.call-done = bf16[256,512]{0,1:T(8,128)(2,1)} async-done(((bf16[2048,512]{0,1:T(8,128)(2,1)}), bf16[256,512]{0,1:T(8,128)(2,1)}) %reduce-scatter.27.cloned.1.call-update) | async-done | bytes 262160 | tf_op jit(solution)/shard_map/reduce_scatter | solution.py:308
  1218.1 35.0 %reduce-scatter.29.cloned.1.call-done = bf16[512,256]{1,0:T(8,128)(2,1)} async-done(((bf16[512,2048]{1,0:T(8,128)(2,1)}), bf16[512,256]{1,0:T(8,128)(2,1)}) %reduce-scatter.29.cloned.1.call-update) | async-done | bytes 262160 | tf_op jit(solution)/shard_map/reduce_scatter | solution.py:311
  1254.8 35.2 %reduce-scatter.23.cloned.1.call-done = bf16[256,512]{0,1:T(8,128)(2,1)} async-done(((bf16[2048,512]{0,1:T(8,128)(2,1)}), bf16[256,512]{0,1:T(8,128)(2,1)}) %reduce-scatter.23.cloned.1.call-update) | async-done | bytes 262160 | tf_op jit(solution)/shard_map/reduce_scatter | solution.py:302
  1291.9 35.2 %reduce-scatter.25.cloned.1.call-done = bf16[256,512]{0,1:T(8,128)(2,1)} async-done(((bf16[2048,512]{0,1:T(8,128)(2,1)}), bf16[256,512]{0,1:T(8,128)(2,1)}) %reduce-scatter.25.cloned.1.call-update) | async-done | bytes 262160 | tf_op jit(solution)/shard_map/reduce_scatter | solution.py:305
  1328.9 52.3 %reduce-scatter.21.cloned.1.call-done = bf16[256,2048]{1,0:T(8,128)(2,1)} async-done(((bf16[1024,2048]{1,0:T(8,128)(2,1)}), bf16[256,2048]{1,0:T(8,128)(2,1)}) %reduce-scatter.21.cloned.1.call-update) | async-done | bytes 1048592 | tf_op jit(solution)/shard_map/reduce_scatter | solution.py:290
  (243 shorter events, 105.4 us)
Async XLA Ops:
  7.2 17.0 %copy-start.43 = (s32[1024]{0:T(1024)S(1)}, s32[1024]{0:T(1024)}, u32[]{:S(2)}) copy-start(s32[1024]{0:T(1024)} %param.18) | copy-start | bytes 12292
  7.2 34.4 %all-gather.22.cloned.1.call-start = ((), (), s32[]{:S(2)}) async-start(), calls=%async_computation.15 | async-start | bytes 2359296 | tf_op jit(solution)/shard_map/all_gather | solution.py:122
  7.9 19.3 %copy-start.50 = (bf16[256]{0:T(256)(128)(2,1)S(1)}, bf16[256]{0:T(256)(128)(2,1)}, u32[]{:S(2)}) copy-start(bf16[256]{0:T(256)(128)(2,1)} %param.26) | copy-start | bytes 1540
  7.9 28.6 %copy-start.42 = (s32[1024]{0:T(1024)S(1)}, s32[1024]{0:T(1024)}, u32[]{:S(2)}) copy-start(s32[1024]{0:T(1024)} %param.17) | copy-start | bytes 12292
  8.0 87.5 %all-gather.16.cloned.1.call-start = ((), (), s32[]{:S(2)}) async-start(), calls=%async_computation.12 | async-start | bytes 5242880 | tf_op jit(solution)/shard_map/all_gather | solution.py:159
  8.7 117.5 %all-gather.20.cloned.1.call-start = ((), (), s32[]{:S(2)}) async-start(), calls=%async_computation.14 | async-start | bytes 2359296 | tf_op jit(solution)/shard_map/all_gather | solution.py:121
  9.4 147.3 %all-gather.18.cloned.1.call-start = ((), (), s32[]{:S(2)}) async-start(), calls=%async_computation.13 | async-start | bytes 2359296 | tf_op jit(solution)/shard_map/all_gather | solution.py:123
  10.0 177.7 %all-gather.24.cloned.1.call-start = ((), (), s32[]{:S(2)}) async-start(), calls=%async_computation.16 | async-start | bytes 2359296 | tf_op jit(solution)/shard_map/all_gather | solution.py:124
  10.6 235.0 %reduce-scatter.15.cloned.1.call-start = ((), (), s32[]{:S(2)}) async-start(), calls=%async_computation.17 | async-start | bytes 5242880 | tf_op jit(solution)/shard_map/reduce_scatter | solution.py:186
  36.4 106.3 %copy-start.35 = (f32[512]{0:T(512)}, f32[512]{0:T(512)S(1)}, u32[]{:S(2)}) copy-start(f32[512]{0:T(512)S(1)} %dynamic-slice_convert_fusion) | copy-start | bytes 6148
  36.5 107.1 %copy-start.37 = (f32[512]{0:T(512)}, f32[512]{0:T(512)S(1)}, u32[]{:S(2)}) copy-start(f32[512]{0:T(512)S(1)} %dynamic-slice_convert_fusion.1) | copy-start | bytes 6148
  100.7 42.1 %copy-start.5 = (f32[1024,512]{0,1:T(8,128)}, f32[1024,512]{0,1:T(8,128)S(1)}, u32[]{:S(2)}) copy-start(f32[1024,512]{0,1:T(8,128)S(1)} %get-tuple-element.152) | copy-start | bytes 6291460
  156.7 14.0 %copy-start.27 = (f32[4,1024]{1,0:T(4,128)}, f32[4,1024]{1,0:T(4,128)S(1)}, u32[]{:S(2)}) copy-start(f32[4,1024]{1,0:T(4,128)S(1)} %get-tuple-element.155) | copy-start | bytes 49156
  162.0 8.8 copy-start.19
  179.1 14.7 %copy-start.53 = (bf16[4,128,1024]{2,1,0:T(8,128)(2,1)}, bf16[4,128,1024]{2,1,0:T(8,128)(2,1)S(1)}, u32[]{:S(2)}) copy-start(bf16[4,128,1024]{2,1,0:T(8,128)(2,1)S(1)} %fusion.41) | copy-start | bytes 3145732
  193.8 53.3 %copy-start.13 = (bf16[256,2048]{1,0:T(8,128)(2,1)S(1)}, bf16[256,2048]{1,0:T(8,128)(2,1)}, u32[]{:S(2)}) copy-start(bf16[256,2048]{1,0:T(8,128)(2,1)} %param.15) | copy-start | bytes 3145732
  193.8 135.4 %all-gather.28.cloned.1.call-start = ((), (), s32[]{:S(2)}) async-start(), calls=%async_computation.19 | async-start | bytes 9437184 | tf_op jit(solution)/shard_map/all_gather | solution.py:125
  194.5 188.2 %all-gather.26.cloned.1.call-start = ((), (), s32[]{:S(2)}) async-start(), calls=%async_computation.18 | async-start | bytes 5242880 | tf_op jit(solution)/shard_map/all_gather | solution.py:195
  249.8 216.6 %all-gather.30.cloned.1.call-start = ((), (), s32[]{:S(2)}) async-start(), calls=%async_computation.20 | async-start | bytes 9437184 | tf_op jit(solution)/shard_map/all_gather | solution.py:126
  250.5 298.3 %all-gather.32.cloned.1.call-start = ((), (), s32[]{:S(2)}) async-start(), calls=%async_computation.21 | async-start | bytes 9437184 | tf_op jit(solution)/shard_map/all_gather | solution.py:127
  251.1 363.4 %reduce-scatter.17.cloned.1.call-start = ((), (), s32[]{:S(2)}) async-start(), calls=%async_computation.22 | async-start | bytes 5242880 | tf_op jit(solution)/shard_map/reduce_scatter | solution.py:201
  562.7 40.5 %copy-start.52 = (bf16[256]{0:T(256)(128)(2,1)S(1)}, bf16[256]{0:T(256)(128)(2,1)}, u32[]{:S(2)}) copy-start(bf16[256]{0:T(256)(128)(2,1)} %param.29) | copy-start | bytes 1540
  562.7 53.3 %copy-start.3 = (bf16[256,2048]{1,0:T(8,128)(2,1)S(1)}, bf16[256,2048]{1,0:T(8,128)(2,1)}, u32[]{:S(2)}) copy-start(bf16[256,2048]{1,0:T(8,128)(2,1)} %reduce-scatter.15.cloned.1.call-done) | copy-start | bytes 3145732
  562.7 113.3 %all-gather.34.cloned.1.call-start = ((), (), s32[]{:S(2)}) async-start(), calls=%async_computation.23 | async-start | bytes 5242880 | tf_op jit(solution)/shard_map/all_gather | solution.py:225
  616.0 5.8 copy-start.16
  621.8 155.4 %copy-start.1 = (f32[256,2048]{1,0:T(8,128)}, f32[256,2048]{1,0:T(8,128)S(1)}, u32[]{:S(2)}) copy-start(f32[256,2048]{1,0:T(8,128)S(1)} %get-tuple-element.121) | copy-start | bytes 6291460
  623.5 151.5 %reduce-scatter.19.cloned.1.call-start = ((), (), s32[]{:S(2)}) async-start(), calls=%async_computation.24 | async-start | bytes 5242880 | tf_op jit(solution)/shard_map/reduce_scatter | solution.py:233
  696.5 12.7 copy-start.55
  722.3 109.3 %all-gather.36.cloned.1.call-start = ((), (), s32[]{:S(2)}) async-start(), calls=%async_computation.25 | async-start | bytes 5242880 | tf_op jit(solution)/shard_map/all_gather | solution.py:248
  778.8 163.9 %reduce-scatter.37.cloned.1.call-start = ((), (), s32[]{:S(2)}) async-start(), calls=%async_computation.34 | async-start | bytes 589824
  836.8 14.6 %slice-start = ((s8[16777216]{0:T(1024)(128)(4,1)}), s8[4194304]{0:T(1024)(128)(4,1)S(1)}, s32[]{:S(2)}) async-start(s8[16777216]{0:T(1024)(128)(4,1)} %bitcast.110), calls=%async_computation.35 | async-start | bytes 8388608
  836.8 14.6 %slice-start.1 = ((s8[16777216]{0:T(1024)(128)(4,1)}), s8[4194304]{0:T(1024)(128)(4,1)S(1)}, s32[]{:S(2)}) async-start(s8[16777216]{0:T(1024)(128)(4,1)} %bitcast.110), calls=%async_computation.36 | async-start | bytes 8388608
  836.8 15.6 %slice-start.2 = ((s8[16777216]{0:T(1024)(128)(4,1)}), s8[4194304]{0:T(1024)(128)(4,1)S(1)}, s32[]{:S(2)}) async-start(s8[16777216]{0:T(1024)(128)(4,1)} %bitcast.110), calls=%async_computation.37 | async-start | bytes 8388608
  836.8 16.7 %slice-start.3 = ((s8[16777216]{0:T(1024)(128)(4,1)}), s8[4194304]{0:T(1024)(128)(4,1)S(1)}, s32[]{:S(2)}) async-start(s8[16777216]{0:T(1024)(128)(4,1)} %bitcast.110), calls=%async_computation.38 | async-start | bytes 8388608
  853.6 8.0 copy-start.12
  877.7 144.2 %reduce-scatter.31.cloned.1.call-start = ((), (), s32[]{:S(2)}) async-start(), calls=%async_computation.31 | async-start | bytes 9437184 | tf_op jit(solution)/shard_map/reduce_scatter | solution.py:91
  892.2 197.3 %reduce-scatter.33.cloned.1.call-start = ((), (), s32[]{:S(2)}) async-start(), calls=%async_computation.32 | async-start | bytes 9437184 | tf_op jit(solution)/shard_map/reduce_scatter | solution.py:94
  906.3 273.0 %reduce-scatter.35.cloned.1.call-start = ((), (), s32[]{:S(2)}) async-start(), calls=%async_computation.33 | async-start | bytes 9437184 | tf_op jit(solution)/shard_map/reduce_scatter | solution.py:97
  920.9 295.3 %reduce-scatter.27.cloned.1.call-start = ((), (), s32[]{:S(2)}) async-start(), calls=%async_computation.29 | async-start | bytes 2359296 | tf_op jit(solution)/shard_map/reduce_scatter | solution.py:308
  921.6 10.1 copy-start.44
  935.5 317.6 %reduce-scatter.29.cloned.1.call-start = ((), (), s32[]{:S(2)}) async-start(), calls=%async_computation.30 | async-start | bytes 2359296 | tf_op jit(solution)/shard_map/reduce_scatter | solution.py:311
  942.7 10.3 copy-start.39
  942.7 347.3 %reduce-scatter.23.cloned.1.call-start = ((), (), s32[]{:S(2)}) async-start(), calls=%async_computation.27 | async-start | bytes 2359296 | tf_op jit(solution)/shard_map/reduce_scatter | solution.py:302
  952.9 3.5 copy-start.45
  960.2 366.8 %reduce-scatter.25.cloned.1.call-start = ((), (), s32[]{:S(2)}) async-start(), calls=%async_computation.28 | async-start | bytes 2359296 | tf_op jit(solution)/shard_map/reduce_scatter | solution.py:305
  967.5 413.8 %reduce-scatter.21.cloned.1.call-start = ((), (), s32[]{:S(2)}) async-start(), calls=%async_computation.26 | async-start | bytes 5242880 | tf_op jit(solution)/shard_map/reduce_scatter | solution.py:290
  1179.3 201.9 %copy-start.15 = (bf16[256,2048]{1,0:T(8,128)(2,1)S(1)}, bf16[256,2048]{1,0:T(8,128)(2,1)}, u32[]{:S(2)}) copy-start(bf16[256,2048]{1,0:T(8,128)(2,1)} %reduce-scatter.19.cloned.1.call-done) | copy-start | bytes 3145732
  1182.1 199.1 %copy-start.2 = (f32[256,2048]{1,0:T(8,128)S(1)}, f32[256,2048]{1,0:T(8,128)}, u32[]{:S(2)}) copy-start(f32[256,2048]{1,0:T(8,128)} %copy-done.1) | copy-start | bytes 6291460
  (35 other events, 58.2 us)
Sparse Core Ops, SparseCore 0:
  9.6 31.9 all-gather.21
  43.4 51.9 all-gather.15
  97.0 29.1 all-gather.19
  127.7 28.5 all-gather.17
  157.7 29.9 all-gather.23
  193.9 51.6 reduce-scatter.14
  247.2 82.0 all-gather.27
  331.6 51.0 all-gather.25
  384.3 82.0 all-gather.29
  467.8 80.9 all-gather.31
  562.8 51.5 reduce-scatter.16
  623.6 52.3 all-gather.33
  722.4 52.5 reduce-scatter.18
  779.0 52.5 all-gather.35
  877.9 31.4 reduce-scatter.36
  911.5 87.6 reduce-scatter.30
  1001.4 88.0 reduce-scatter.32
  1091.6 87.6 reduce-scatter.34
  1181.6 34.5 reduce-scatter.26
  1218.3 34.6 reduce-scatter.28
  1255.3 34.5 reduce-scatter.22
  1292.3 34.6 reduce-scatter.24
  1330.0 51.1 reduce-scatter.20
where the time goes:
time: 1400 us; the launch traced here: 1390 us
  waiting for transfers between devices  903 us (64%)
  matrix products  238 us (17%)
  blocking collectives  144 us (10%)
  other arithmetic  62 us (4%)
  local copies, waits for them, and re-layouts  26.9 us (2%)
  between operations  17.5 us (1%)
    reduce_scatter x1, waiting for transfers between devices, reduce_ffn(): lax.psum_scatter(weight_down.astype(jnp.bfloat16), 'dp', scatter_dimensio...  87.1 us
    psum x2, blocking collectives, on_device(): lax.psum((jnp.sum(valid * error * error), jnp.sum(valid)), ('dp', 'tensor'))  79.8 us
    all_gather x1, waiting for transfers between devices, on_device(): lax.all_gather(wg, 'dp', axis=0, tiled=True)  78.1 us
    all_gather x1, waiting for transfers between devices, on_device(): lax.all_gather(wu, 'dp', axis=0, tiled=True)  68.9 us
    all_gather x1, waiting for transfers between devices, on_device(): lax.all_gather(wd, 'dp', axis=1, tiled=True)  65.5 us
    reduce_scatter x1, waiting for transfers between devices, reduce_ffn(): lax.psum_scatter(weight_up.astype(jnp.bfloat16), 'dp', scatter_dimension=...  64.7 us
    dot_general x7, matrix products, times_transposed(): lax.dot_general(left, right, (((1,), (1,)), ((), ())), preferred_element_...  62.3 us
    dot_general x7, matrix products, inner_rows(): lax.dot_general(left, right, (((0,), (0,)), ((), ())), preferred_element_...  60.1 us
  transfers between devices with their start and end apart: 23, of which 20 were waited for; matrix products, arithmetic and copies ran while one was open for 14% of the time, Pallas kernels for 0%

commit v1 on v0

--- a/solution.py
+++ b/solution.py
@@ -192,7 +192,12 @@
     scale_attn = lax.rsqrt(jnp.mean(branch_attn * branch_attn, axis=1, keepdims=True) + EPS)
     normed_attn = branch_attn * scale_attn
     resid = inputs.astype(jnp.float32) + normed_attn * norm_gain_attn
-    whole_h = lax.all_gather(resid.astype(jnp.bfloat16), "tensor", axis=0, tiled=True)
+    whole_h = jnp.concatenate(
+        lax.all_to_all(
+            jnp.stack([resid.astype(jnp.bfloat16)] * lax.axis_size("tensor")), "tensor", 0, 0
+        ),
+        axis=0,
+    )
     gate = jnp.dot(whole_h, full_gate, preferred_element_type=jnp.float32)
     up = jnp.dot(whole_h, full_up, preferred_element_type=jnp.float32)
     sigma = jax.nn.sigmoid(gate)

time: 1400 us -> 1350 us (0.964)
  waiting for transfers between devices: 903 us -> 841 us
    all_gather x1 -> x0, waiting for transfers between devices: 53.5 us -> none  [on_device(): lax.all_gather(resid.astype(jnp.bfloat16), 'tensor', axis=0, tiled=True)]
  transfers between devices with their start and end apart: 23 -> 23, of which waited for: 20 -> 19; matrix products, arithmetic and copies ran while one was open for 14% -> 14% of each run, Pallas kernels for 0% -> 0%
where the time goes in v1:
time: 1350 us; the launch traced here: 1340 us
  waiting for transfers between devices  841 us (62%)
  matrix products  238 us (18%)
  blocking collectives  144 us (11%)
  other arithmetic  61.2 us (5%)
  local copies, waits for them, and re-layouts  29.4 us (2%)
  between operations  17.8 us (1%)
    reduce_scatter x1, waiting for transfers between devices, reduce_ffn(): lax.psum_scatter(weight_down.astype(jnp.bfloat16), 'dp', scatter_dimensio...  87 us
    psum x2, blocking collectives, on_device(): lax.psum((jnp.sum(valid * error * error), jnp.sum(valid)), ('dp', 'tensor'))  79.8 us
    all_gather x1, waiting for transfers between devices, on_device(): lax.all_gather(wg, 'dp', axis=0, tiled=True)  72.8 us
    all_gather x1, waiting for transfers between devices, on_device(): lax.all_gather(wu, 'dp', axis=0, tiled=True)  67.5 us
    all_gather x1, waiting for transfers between devices, on_device(): lax.all_gather(wd, 'dp', axis=1, tiled=True)  65.6 us
    reduce_scatter x1, waiting for transfers between devices, reduce_ffn(): lax.psum_scatter(weight_up.astype(jnp.bfloat16), 'dp', scatter_dimension=...  64.7 us
    dot_general x7, matrix products, times_transposed(): lax.dot_general(left, right, (((1,), (1,)), ((), ())), preferred_element_...  62.3 us
    dot_general x7, matrix products, inner_rows(): lax.dot_general(left, right, (((0,), (0,)), ((), ())), preferred_element_...  60.1 us
  transfers between devices with their start and end apart: 23, of which 19 were waited for; matrix products, arithmetic and copies ran while one was open for 14% of the time, Pallas kernels for 0%

profile of v1, /device:TPU:0, one launch (start us, length us, event | category | flops | bytes accessed | tf_op | source)
XLA Modules:
  0.0 1337.2 jit_solution(17056650839619746163)
XLA Ops:
  10.7 13.5 %all-gather.1 = bf16[8,1,256]{2,1,0:T(2,128)(2,1)S(1)} all-gather(bf16[1,1,256]{2,1,0:T(2,128)(2,1)S(1)} %reshape.231), channel_id=1, replica_groups=mesh['dp'=8,'tensor'=4] {'dp'}, dimensions={0}, use_global_device_ids=true | all-gather | bytes 4608 | tf_op jit(solution)/shard_map/all_gather | solution.py:129
  27.2 9.1 all-gather
  41.6 53.8 %all-gather.15.cloned.1.call-done = bf16[1024,2048]{1,0:T(8,128)(2,1)} async-done(((bf16[256,2048]{1,0:T(8,128)(2,1)}), bf16[1024,2048]{1,0:T(8,128)(2,1)}) %all-gather.15.cloned.1.call-update) | async-done | bytes 4194320 | tf_op jit(solution)/shard_map/all_gather | solution.py:159
  95.4 5.3 multiply_reduce_fusion.3
  100.7 25.5 %all-gather.19.cloned.1.call-done = bf16[2048,512]{1,0:T(8,128)(2,1)} async-done(((bf16[256,512]{1,0:T(8,128)(2,1)}), bf16[2048,512]{1,0:T(8,128)(2,1)}) %all-gather.19.cloned.1.call-update) | async-done | bytes 2097168 | tf_op jit(solution)/shard_map/all_gather | solution.py:121
  126.2 6.6 multiply_reduce_fusion.4
  132.8 10.0 all-reduce
  149.0 7.7 fusion.52
  156.7 5.2 convolution_convert_fusion.10
  162.0 8.7 fusion
  171.3 7.7 fusion.41
  179.1 8.7 all-gather.23.cloned.1.call-done
  187.7 6.0 convolution_convert_fusion.4
  196.0 11.7 all-gather.2
  207.7 37.8 %reduce-scatter.15.cloned.1.call-done = bf16[256,2048]{1,0:T(8,128)(2,1)} async-done(((bf16[1024,2048]{1,0:T(8,128)(2,1)}), bf16[256,2048]{1,0:T(8,128)(2,1)}) %reduce-scatter.15.cloned.1.call-update) | async-done | bytes 1048592 | tf_op jit(solution)/shard_map/reduce_scatter | solution.py:186
  256.4 72.8 %all-gather.25.cloned.1.call-done = bf16[2048,2048]{1,0:T(8,128)(2,1)} async-done(((bf16[256,2048]{1,0:T(8,128)(2,1)}), bf16[2048,2048]{1,0:T(8,128)(2,1)}) %all-gather.25.cloned.1.call-update) | async-done | bytes 8388624 | tf_op jit(solution)/shard_map/all_gather | solution.py:125
  329.2 14.7 %fusion.53 = f32[1024,2048]{1,0:T(8,128)} fusion(bf16[1024,2048]{1,0:T(8,128)(2,1)} %bitcast.6, bf16[2048,2048]{1,0:T(8,128)(2,1)} %all-gather.25.cloned.1.call-done), kind=kOutput, calls=%fused_computation.129 | convolution fusion | flops 8589934592 | bytes 20971520 | tf_op jit(solution)/shard_map/dot_general | solution.py:201
  343.8 67.5 %all-gather.27.cloned.1.call-done = bf16[2048,2048]{1,0:T(8,128)(2,1)} async-done(((bf16[256,2048]{1,0:T(8,128)(2,1)}), bf16[2048,2048]{1,0:T(8,128)(2,1)}) %all-gather.27.cloned.1.call-update) | async-done | bytes 8388624 | tf_op jit(solution)/shard_map/all_gather | solution.py:126
  411.3 17.0 %multiply_convert_fusion.3 = (bf16[1024,2048]{1,0:T(8,128)(2,1)}, f32[1024,2048]{1,0:T(8,128)}) fusion(f32[1024,2048]{1,0:T(8,128)} %fusion.53, bf16[1024,2048]{1,0:T(8,128)(2,1)} %bitcast.6, bf16[2048,2048]{1,0:T(8,128)(2,1)} %all-gather.27.cloned.1.call-done), kind=kOutput, calls=%fused_computation.14 | convolution fusion | flops 8602517504 | bytes 33554432 | tf_op jit(solution)/shard_map/dot_general | solution.py:202
  428.3 65.6 %all-gather.29.cloned.1.call-done = bf16[2048,2048]{1,0:T(8,128)(2,1)} async-done(((bf16[2048,256]{1,0:T(8,128)(2,1)}), bf16[2048,2048]{1,0:T(8,128)(2,1)}) %all-gather.29.cloned.1.call-update) | async-done | bytes 8388624 | tf_op jit(solution)/shard_map/all_gather | solution.py:127
  493.9 13.9 %convolution_convert_fusion.3 = bf16[1024,2048]{1,0:T(8,128)(2,1)} fusion(bf16[1024,2048]{1,0:T(8,128)(2,1)} %get-tuple-element.157, bf16[2048,2048]{1,0:T(8,128)(2,1)} %all-gather.29.cloned.1.call-done), kind=kOutput, calls=%fused_computation.23 | convolution fusion | flops 8592031744 | bytes 16777216 | tf_op jit(solution)/shard_map/dot_general | solution.py:207
  508.5 39.7 %psum.52 = f32[]{:T(128)} all-reduce(f32[]{:T(128)} %get-tuple-element.150), channel_id=1, replica_groups=mesh['dp'=8,'tensor'=4] {'dp','tensor'}, use_global_device_ids=true, to_apply=%region_13.14 | all-reduce | flops 1 | bytes 8 | tf_op jit(solution)/shard_map/psum | solution.py:218
  548.2 10.7 all-gather.3
  561.1 5.8 fusion.31
  568.6 52.5 %all-gather.31.cloned.1.call-done = bf16[1024,2048]{1,0:T(8,128)(2,1)} async-done(((bf16[256,2048]{1,0:T(8,128)(2,1)}), bf16[1024,2048]{1,0:T(8,128)(2,1)}) %all-gather.31.cloned.1.call-update) | async-done | bytes 4194320 | tf_op jit(solution)/shard_map/all_gather | solution.py:230
  621.1 20.5 %multiply_convert_fusion.1 = (bf16[1024,2048]{1,0:T(8,128)(2,1)}, bf16[1024,2048]{1,0:T(8,128)(2,1)}) fusion(f32[1024,2048]{1,0:T(8,128)} %fusion.53, f32[1024,2048]{1,0:T(8,128)} %get-tuple-element.158, bf16[1024,2048]{1,0:T(8,128)(2,1)} %all-gather.31.cloned.1.call-done, bf16[2048,2048]{1,0:T(8,128)(2,1)} %all-gather.29.cloned.1.call-done), kind=kOutput, calls=%fused_computation.12 | convolution fusion | flops 8617197568 | bytes 37748736 | tf_op jit(solution)/shard_map/dot_general | solution.py:39
  641.6 12.7 fusion.54
  654.3 13.1 add_convert_fusion.1
  667.5 52.7 %reduce-scatter.19.cloned.1.call-done = bf16[256,2048]{1,0:T(8,128)(2,1)} async-done(((bf16[1024,2048]{1,0:T(8,128)(2,1)}), bf16[256,2048]{1,0:T(8,128)(2,1)}) %reduce-scatter.19.cloned.1.call-update) | async-done | bytes 1048592 | tf_op jit(solution)/shard_map/reduce_scatter | solution.py:238
  725.9 50.8 %all-gather.33.cloned.1.call-done = bf16[1024,2048]{1,0:T(8,128)(2,1)} async-done(((bf16[256,2048]{1,0:T(8,128)(2,1)}), bf16[1024,2048]{1,0:T(8,128)(2,1)}) %all-gather.33.cloned.1.call-update) | async-done | bytes 4194320 | tf_op jit(solution)/shard_map/all_gather | solution.py:253
  782.0 14.5 %multiply_reduce_fusion = (f32[4,1024]{1,0:T(4,128)}, f32[4,1024,1024]{1,2,0:T(8,128)}) fusion(f32[4,1024,1024]{1,2,0:T(8,128)} %get-tuple-element.156, f32[4,1024]{1,0:T(4,128)} %log_add_fusion, bf16[1024,4,128]{0,2,1:T(8,128)(2,1)S(1)} %bitcast.117, bf16[1024,4,128]{0,2,1:T(8,128)(2,1)} %bitcast.122), kind=kOutput, calls=%fused_computation.1 | convolution fusion | flops 1086320640 | bytes 35684352 | tf_op jit(solution)/shard_map/while/body/eval_jaxpr/qhd,khd->hqk/dot_general | solution.py:73
  798.8 8.0 multiply_convert_fusion
  810.1 6.4 bitcast_multiply_fusion.2
  823.0 14.4 %convolution_convert_fusion.2 = bf16[2048,2048]{1,0:T(8,128)(2,1)} fusion(bf16[1024,2048]{1,0:T(8,128)(2,1)} %bitcast.6, bf16[1024,2048]{1,0:T(8,128)(2,1)} %get-tuple-element.125), kind=kOutput, calls=%fused_computation.20 | convolution fusion | flops 8594128896 | bytes 16777216 | tf_op jit(solution)/shard_map/dot_general | solution.py:33
  837.4 14.1 %convolution_convert_fusion.1 = bf16[2048,2048]{1,0:T(8,128)(2,1)} fusion(bf16[1024,2048]{1,0:T(8,128)(2,1)} %bitcast.6, bf16[1024,2048]{1,0:T(8,128)(2,1)} %get-tuple-element.124), kind=kOutput, calls=%fused_computation.19 | convolution fusion | flops 8594128896 | bytes 16777216 | tf_op jit(solution)/shard_map/dot_general | solution.py:33
  851.5 14.5 %convolution_convert_fusion = bf16[2048,2048]{1,0:T(8,128)(2,1)} fusion(bf16[1024,2048]{1,0:T(8,128)(2,1)} %get-tuple-element.157, bf16[1024,2048]{1,0:T(8,128)(2,1)} %all-gather.31.cloned.1.call-done), kind=kOutput, calls=%fused_computation.18 | convolution fusion | flops 8594128896 | bytes 16777216 | tf_op jit(solution)/shard_map/dot_general | solution.py:33
  866.8 9.1 fusion.42
  881.9 6.0 convolution_convert_fusion.5
  888.9 9.2 all-reduce.1
  919.1 6.0 add_convert_fusion
  925.8 40.1 %psum.51 = f32[]{:T(128)} all-reduce(f32[]{:T(128)} %get-tuple-element.115), channel_id=1, replica_groups=mesh['dp'=8,'tensor'=4] {'dp','tensor'}, use_global_device_ids=true, to_apply=%region_11.12 | all-reduce | flops 1 | bytes 8 | tf_op jit(solution)/shard_map/psum | solution.py:218
  969.9 64.7 %reduce-scatter.33.cloned.1.call-done = bf16[256,2048]{1,0:T(8,128)(2,1)} async-done(((bf16[2048,2048]{1,0:T(8,128)(2,1)}), bf16[256,2048]{1,0:T(8,128)(2,1)}) %reduce-scatter.33.cloned.1.call-update) | async-done | bytes 1048592 | tf_op jit(solution)/shard_map/reduce_scatter | solution.py:94
  1037.4 87.0 %reduce-scatter.35.cloned.1.call-done = bf16[2048,256]{1,0:T(8,128)(2,1)} async-done(((bf16[2048,2048]{1,0:T(8,128)(2,1)}), bf16[2048,256]{1,0:T(8,128)(2,1)}) %reduce-scatter.35.cloned.1.call-update) | async-done | bytes 1048592 | tf_op jit(solution)/shard_map/reduce_scatter | solution.py:97
  1127.3 33.9 %reduce-scatter.27.cloned.1.call-done = bf16[256,512]{0,1:T(8,128)(2,1)} async-done(((bf16[2048,512]{0,1:T(8,128)(2,1)}), bf16[256,512]{0,1:T(8,128)(2,1)}) %reduce-scatter.27.cloned.1.call-update) | async-done | bytes 262160 | tf_op jit(solution)/shard_map/reduce_scatter | solution.py:313
  1163.1 35.1 %reduce-scatter.29.cloned.1.call-done = bf16[512,256]{1,0:T(8,128)(2,1)} async-done(((bf16[512,2048]{1,0:T(8,128)(2,1)}), bf16[512,256]{1,0:T(8,128)(2,1)}) %reduce-scatter.29.cloned.1.call-update) | async-done | bytes 262160 | tf_op jit(solution)/shard_map/reduce_scatter | solution.py:316
  1199.9 35.1 %reduce-scatter.23.cloned.1.call-done = bf16[256,512]{0,1:T(8,128)(2,1)} async-done(((bf16[2048,512]{0,1:T(8,128)(2,1)}), bf16[256,512]{0,1:T(8,128)(2,1)}) %reduce-scatter.23.cloned.1.call-update) | async-done | bytes 262160 | tf_op jit(solution)/shard_map/reduce_scatter | solution.py:307
  1236.9 35.1 %reduce-scatter.25.cloned.1.call-done = bf16[256,512]{0,1:T(8,128)(2,1)} async-done(((bf16[2048,512]{0,1:T(8,128)(2,1)}), bf16[256,512]{0,1:T(8,128)(2,1)}) %reduce-scatter.25.cloned.1.call-update) | async-done | bytes 262160 | tf_op jit(solution)/shard_map/reduce_scatter | solution.py:310
  1273.9 52.2 %reduce-scatter.21.cloned.1.call-done = bf16[256,2048]{1,0:T(8,128)(2,1)} async-done(((bf16[1024,2048]{1,0:T(8,128)(2,1)}), bf16[256,2048]{1,0:T(8,128)(2,1)}) %reduce-scatter.21.cloned.1.call-update) | async-done | bytes 1048592 | tf_op jit(solution)/shard_map/reduce_scatter | solution.py:295
  (243 shorter events, 106.9 us)
Async XLA Ops:
  7.2 17.0 %copy-start.43 = (s32[1024]{0:T(1024)S(1)}, s32[1024]{0:T(1024)}, u32[]{:S(2)}) copy-start(s32[1024]{0:T(1024)} %param.18) | copy-start | bytes 12292
  7.2 34.4 %all-gather.21.cloned.1.call-start = ((), (), s32[]{:S(2)}) async-start(), calls=%async_computation.16 | async-start | bytes 2359296 | tf_op jit(solution)/shard_map/all_gather | solution.py:122
  7.9 19.3 %copy-start.50 = (bf16[256]{0:T(256)(128)(2,1)S(1)}, bf16[256]{0:T(256)(128)(2,1)}, u32[]{:S(2)}) copy-start(bf16[256]{0:T(256)(128)(2,1)} %param.26) | copy-start | bytes 1540
  7.9 28.6 %copy-start.42 = (s32[1024]{0:T(1024)S(1)}, s32[1024]{0:T(1024)}, u32[]{:S(2)}) copy-start(s32[1024]{0:T(1024)} %param.17) | copy-start | bytes 12292
  8.0 87.5 %all-gather.15.cloned.1.call-start = ((), (), s32[]{:S(2)}) async-start(), calls=%async_computation.13 | async-start | bytes 5242880 | tf_op jit(solution)/shard_map/all_gather | solution.py:159
  8.7 117.5 %all-gather.19.cloned.1.call-start = ((), (), s32[]{:S(2)}) async-start(), calls=%async_computation.15 | async-start | bytes 2359296 | tf_op jit(solution)/shard_map/all_gather | solution.py:121
  9.4 147.3 %all-gather.17.cloned.1.call-start = ((), (), s32[]{:S(2)}) async-start(), calls=%async_computation.14 | async-start | bytes 2359296 | tf_op jit(solution)/shard_map/all_gather | solution.py:123
  10.0 177.7 %all-gather.23.cloned.1.call-start = ((), (), s32[]{:S(2)}) async-start(), calls=%async_computation.17 | async-start | bytes 2359296 | tf_op jit(solution)/shard_map/all_gather | solution.py:124
  10.6 234.9 %reduce-scatter.15.cloned.1.call-start = ((), (), s32[]{:S(2)}) async-start(), calls=%async_computation.18 | async-start | bytes 5242880 | tf_op jit(solution)/shard_map/reduce_scatter | solution.py:186
  36.4 106.3 %copy-start.35 = (f32[512]{0:T(512)}, f32[512]{0:T(512)S(1)}, u32[]{:S(2)}) copy-start(f32[512]{0:T(512)S(1)} %dynamic-slice_convert_fusion) | copy-start | bytes 6148
  36.5 107.1 %copy-start.37 = (f32[512]{0:T(512)}, f32[512]{0:T(512)S(1)}, u32[]{:S(2)}) copy-start(f32[512]{0:T(512)S(1)} %dynamic-slice_convert_fusion.1) | copy-start | bytes 6148
  100.7 42.1 %copy-start.5 = (f32[1024,512]{0,1:T(8,128)}, f32[1024,512]{0,1:T(8,128)S(1)}, u32[]{:S(2)}) copy-start(f32[1024,512]{0,1:T(8,128)S(1)} %get-tuple-element.152) | copy-start | bytes 6291460
  156.7 14.0 %copy-start.27 = (f32[4,1024]{1,0:T(4,128)}, f32[4,1024]{1,0:T(4,128)S(1)}, u32[]{:S(2)}) copy-start(f32[4,1024]{1,0:T(4,128)S(1)} %get-tuple-element.155) | copy-start | bytes 49156
  162.0 8.8 copy-start.19
  179.1 14.6 %copy-start.53 = (bf16[4,128,1024]{2,1,0:T(8,128)(2,1)}, bf16[4,128,1024]{2,1,0:T(8,128)(2,1)S(1)}, u32[]{:S(2)}) copy-start(bf16[4,128,1024]{2,1,0:T(8,128)(2,1)S(1)} %fusion.41) | copy-start | bytes 3145732
  193.7 53.3 %copy-start.13 = (bf16[256,2048]{1,0:T(8,128)(2,1)S(1)}, bf16[256,2048]{1,0:T(8,128)(2,1)}, u32[]{:S(2)}) copy-start(bf16[256,2048]{1,0:T(8,128)(2,1)} %param.15) | copy-start | bytes 3145732
  193.7 135.4 %all-gather.25.cloned.1.call-start = ((), (), s32[]{:S(2)}) async-start(), calls=%async_computation.19 | async-start | bytes 9437184 | tf_op jit(solution)/shard_map/all_gather | solution.py:125
  194.5 216.8 %all-gather.27.cloned.1.call-start = ((), (), s32[]{:S(2)}) async-start(), calls=%async_computation.20 | async-start | bytes 9437184 | tf_op jit(solution)/shard_map/all_gather | solution.py:126
  195.2 298.7 %all-gather.29.cloned.1.call-start = ((), (), s32[]{:S(2)}) async-start(), calls=%async_computation.21 | async-start | bytes 9437184 | tf_op jit(solution)/shard_map/all_gather | solution.py:127
  251.3 77.8 %all-to-all-start = ((bf16[4,256,2048]{2,1,0:T(8,128)(2,1)}), bf16[4,256,2048]{2,1,0:T(8,128)(2,1)}, u32[]{:S(2)}, u32[]{:S(2)}) async-start(bf16[4,256,2048]{2,1,0:T(8,128)(2,1)} %stack.27), calls=%async_computation.1 | async-start | bytes 8388608 | tf_op jit(solution)/shard_map/all_to_all | solution.py:196
  256.3 303.2 %reduce-scatter.17.cloned.1.call-start = ((), (), s32[]{:S(2)}) async-start(), calls=%async_computation.22 | async-start | bytes 5242880 | tf_op jit(solution)/shard_map/reduce_scatter | solution.py:206
  507.8 40.5 %copy-start.52 = (bf16[256]{0:T(256)(128)(2,1)S(1)}, bf16[256]{0:T(256)(128)(2,1)}, u32[]{:S(2)}) copy-start(bf16[256]{0:T(256)(128)(2,1)} %param.29) | copy-start | bytes 1540
  507.8 53.3 %copy-start.3 = (bf16[256,2048]{1,0:T(8,128)(2,1)S(1)}, bf16[256,2048]{1,0:T(8,128)(2,1)}, u32[]{:S(2)}) copy-start(bf16[256,2048]{1,0:T(8,128)(2,1)} %reduce-scatter.15.cloned.1.call-done) | copy-start | bytes 3145732
  507.8 113.3 %all-gather.31.cloned.1.call-start = ((), (), s32[]{:S(2)}) async-start(), calls=%async_computation.23 | async-start | bytes 5242880 | tf_op jit(solution)/shard_map/all_gather | solution.py:230
  561.1 5.8 copy-start.16
  566.9 155.4 %copy-start.1 = (f32[256,2048]{1,0:T(8,128)}, f32[256,2048]{1,0:T(8,128)S(1)}, u32[]{:S(2)}) copy-start(f32[256,2048]{1,0:T(8,128)S(1)} %get-tuple-element.121) | copy-start | bytes 6291460
  568.6 151.6 %reduce-scatter.19.cloned.1.call-start = ((), (), s32[]{:S(2)}) async-start(), calls=%async_computation.24 | async-start | bytes 5242880 | tf_op jit(solution)/shard_map/reduce_scatter | solution.py:238
  641.6 12.7 copy-start.55
  667.4 109.3 %all-gather.33.cloned.1.call-start = ((), (), s32[]{:S(2)}) async-start(), calls=%async_computation.25 | async-start | bytes 5242880 | tf_op jit(solution)/shard_map/all_gather | solution.py:253
  724.0 163.9 %reduce-scatter.37.cloned.1.call-start = ((), (), s32[]{:S(2)}) async-start(), calls=%async_computation.34 | async-start | bytes 589824
  782.0 14.6 %slice-start = ((s8[16777216]{0:T(1024)(128)(4,1)}), s8[4194304]{0:T(1024)(128)(4,1)S(1)}, s32[]{:S(2)}) async-start(s8[16777216]{0:T(1024)(128)(4,1)} %bitcast.111), calls=%async_computation.35 | async-start | bytes 8388608
  782.0 14.6 %slice-start.1 = ((s8[16777216]{0:T(1024)(128)(4,1)}), s8[4194304]{0:T(1024)(128)(4,1)S(1)}, s32[]{:S(2)}) async-start(s8[16777216]{0:T(1024)(128)(4,1)} %bitcast.111), calls=%async_computation.36 | async-start | bytes 8388608
  782.0 15.6 %slice-start.2 = ((s8[16777216]{0:T(1024)(128)(4,1)}), s8[4194304]{0:T(1024)(128)(4,1)S(1)}, s32[]{:S(2)}) async-start(s8[16777216]{0:T(1024)(128)(4,1)} %bitcast.111), calls=%async_computation.37 | async-start | bytes 8388608
  782.0 16.7 %slice-start.3 = ((s8[16777216]{0:T(1024)(128)(4,1)}), s8[4194304]{0:T(1024)(128)(4,1)S(1)}, s32[]{:S(2)}) async-start(s8[16777216]{0:T(1024)(128)(4,1)} %bitcast.111), calls=%async_computation.38 | async-start | bytes 8388608
  798.8 8.0 copy-start.12
  822.9 144.2 %reduce-scatter.31.cloned.1.call-start = ((), (), s32[]{:S(2)}) async-start(), calls=%async_computation.31 | async-start | bytes 9437184 | tf_op jit(solution)/shard_map/reduce_scatter | solution.py:91
  837.4 197.3 %reduce-scatter.33.cloned.1.call-start = ((), (), s32[]{:S(2)}) async-start(), calls=%async_computation.32 | async-start | bytes 9437184 | tf_op jit(solution)/shard_map/reduce_scatter | solution.py:94
  851.5 273.0 %reduce-scatter.35.cloned.1.call-start = ((), (), s32[]{:S(2)}) async-start(), calls=%async_computation.33 | async-start | bytes 9437184 | tf_op jit(solution)/shard_map/reduce_scatter | solution.py:97
  866.1 295.1 %reduce-scatter.27.cloned.1.call-start = ((), (), s32[]{:S(2)}) async-start(), calls=%async_computation.29 | async-start | bytes 2359296 | tf_op jit(solution)/shard_map/reduce_scatter | solution.py:313
  866.8 10.1 copy-start.44
  880.7 317.5 %reduce-scatter.29.cloned.1.call-start = ((), (), s32[]{:S(2)}) async-start(), calls=%async_computation.30 | async-start | bytes 2359296 | tf_op jit(solution)/shard_map/reduce_scatter | solution.py:316
  887.8 10.3 copy-start.39
  887.9 347.2 %reduce-scatter.23.cloned.1.call-start = ((), (), s32[]{:S(2)}) async-start(), calls=%async_computation.27 | async-start | bytes 2359296 | tf_op jit(solution)/shard_map/reduce_scatter | solution.py:307
  898.1 3.5 copy-start.45
  905.4 366.6 %reduce-scatter.25.cloned.1.call-start = ((), (), s32[]{:S(2)}) async-start(), calls=%async_computation.28 | async-start | bytes 2359296 | tf_op jit(solution)/shard_map/reduce_scatter | solution.py:310
  912.6 413.4 %reduce-scatter.21.cloned.1.call-start = ((), (), s32[]{:S(2)}) async-start(), calls=%async_computation.26 | async-start | bytes 5242880 | tf_op jit(solution)/shard_map/reduce_scatter | solution.py:295
  1124.5 201.6 %copy-start.15 = (bf16[256,2048]{1,0:T(8,128)(2,1)S(1)}, bf16[256,2048]{1,0:T(8,128)(2,1)}, u32[]{:S(2)}) copy-start(bf16[256,2048]{1,0:T(8,128)(2,1)} %reduce-scatter.19.cloned.1.call-done) | copy-start | bytes 3145732
  1127.3 198.8 %copy-start.2 = (f32[256,2048]{1,0:T(8,128)S(1)}, f32[256,2048]{1,0:T(8,128)}, u32[]{:S(2)}) copy-start(f32[256,2048]{1,0:T(8,128)} %copy-done.1) | copy-start | bytes 6291460
  (35 other events, 59.6 us)
Sparse Core Ops, SparseCore 0:
  9.6 31.9 all-gather.20
  43.4 51.9 all-gather.14
  97.0 29.1 all-gather.18
  127.7 28.5 all-gather.16
  157.7 29.9 all-gather.22
  193.8 51.6 reduce-scatter.14
  247.1 82.0 all-gather.24
  330.8 80.5 all-gather.26
  412.9 80.9 all-gather.28
  507.9 51.5 reduce-scatter.16
  568.7 52.3 all-gather.30
  667.5 52.5 reduce-scatter.18
  724.1 52.5 all-gather.32
  823.0 31.4 reduce-scatter.36
  856.7 87.6 reduce-scatter.30
  946.6 88.0 reduce-scatter.32
  1036.8 87.6 reduce-scatter.34
  1126.6 34.5 reduce-scatter.26
  1163.5 34.6 reduce-scatter.28
  1200.3 34.6 reduce-scatter.22
  1237.3 34.6 reduce-scatter.24
  1275.0 51.0 reduce-scatter.20
